TPU v7x, 256 devices: a whole 4x4x8 slice. The times are simulated.
256 devices in a mesh: slab: 32 (over z, y), snap: 8 (over x, core).
Axes of the slice: x: 4, y: 4, z: 8, core: 2. Of those that a mesh axis runs over, the one named last changes fastest.
Arguments:
- flow: bfloat16 [128, 3, 64, 64, 128], P('snap', None, 'slab'), may hold values from -127 to 127
- large_scale: bfloat16 [3, 64, 64, 128], P(None, 'slab'), may hold values from -6 to 6
- modulation: float32 [128, 64], replicated, may hold values from -15 to 15
- metric: float32 [4, 64, 64, 128], P(None, 'slab'), may hold values from -0.5 to 9.6
Outputs:
- whitened: float32 [128, 3, 64, 64, 128], P(None, None, 'slab', 'snap')
All inputs are finite; a program needn't handle non-finite values.
Results may differ from a plain program's by a relative error of at most 0.0003.
Values may be sent and summed in bfloat16 or wider, within the bound.
A program may use at most 64 MiB of HBM per device.

v0:
```python
import jax
import jax.numpy as jnp
from jax import lax
from jax.sharding import PartitionSpec as P

NSITER = 6


def with_halo(block, sides, width):
    for axis, dim in sides:
        count = lax.axis_size(axis)
        forward = [(i, i + 1) for i in range(count - 1)]
        backward = [(target, source) for source, target in forward]
        low = lax.ppermute(
            lax.slice_in_dim(block, block.shape[dim] - width, None, axis=dim), axis, forward
        )
        high = lax.ppermute(lax.slice_in_dim(block, 0, width, axis=dim), axis, backward)
        block = jnp.concatenate([low, block, high], axis=dim)
    return block


def vorticity(velocity, metric):
    metric_x = metric[0]
    shear_xy = metric[1]
    metric_y = metric[2]
    metric_z = metric[3]

    def along_x(values):
        return 0.5 * (values[..., 1:-1, 2:, :] - values[..., 1:-1, :-2, :])

    def along_y(values):
        return 0.5 * (values[..., 2:, 1:-1, :] - values[..., :-2, 1:-1, :])

    def along_z(values):
        center = values[..., 1:-1, 1:-1, :]
        return 0.5 * (jnp.roll(center, -1, -1) - jnp.roll(center, 1, -1))

    def slope_x(values):
        return metric_x * along_x(values) + shear_xy * along_y(values)

    def slope_y(values):
        return metric_y * along_y(values)

    def slope_z(values):
        return metric_z * along_z(values)

    stream = velocity[..., 0, :, :, :]
    normal = velocity[..., 1, :, :, :]
    spanwise = velocity[..., 2, :, :, :]
    around_x = slope_y(spanwise) - slope_z(normal)
    around_y = slope_z(stream) - slope_x(spanwise)
    around_z = slope_x(normal) - slope_y(stream)
    return jnp.stack([around_x, around_y, around_z], axis=-4)


def wrap_columns(values):
    return jnp.concatenate([values[..., -1:, :], values, values[..., :1, :]], axis=-2)


def whitening(correlation):
    identity = jnp.eye(correlation.shape[0], dtype=correlation.dtype)
    frob_scale = jnp.sqrt(jnp.sum(correlation * correlation) + 1e-06)
    approx = correlation / frob_scale
    inverse = identity
    for repeat in range(NSITER):
        factor = 0.5 * (3.0 * identity - jnp.dot(inverse, approx, precision=lax.Precision.HIGHEST))
        approx = jnp.dot(approx, factor, precision=lax.Precision.HIGHEST)
        inverse = jnp.dot(factor, inverse, precision=lax.Precision.HIGHEST)
    return inverse / jnp.sqrt(frob_scale)


def inner_rows(left_rows, right_rows):
    return lax.dot_general(
        left_rows,
        right_rows,
        (((1,), (1,)), ((), ())),
        precision=lax.Precision.HIGHEST,
        preferred_element_type=jnp.float32,
    )


def planes_padded(flow, large_scale):
    joined = jnp.concatenate([flow, large_scale[None]], axis=0)
    return with_halo(joined, (("slab", 2),), 1)


def per_device(flow, large_scale, modulation, metric):
    snap_count = lax.axis_size("snap")
    slab_count = lax.axis_size("slab")
    own_snaps = flow.shape[0]
    block_cols = flow.shape[3] // snap_count
    snap_index = lax.axis_index("snap")
    mod_ext = jnp.concatenate([modulation[:, -1:], modulation, modulation[:, :1]], axis=1)
    padded = planes_padded(flow, large_scale)
    large_ext = wrap_columns(padded[own_snaps].astype(jnp.float32))
    mod_mine = lax.dynamic_slice_in_dim(mod_ext, snap_index * own_snaps, own_snaps, 0)
    velocity = (
        wrap_columns(padded[:own_snaps].astype(jnp.float32))
        + mod_mine[:, None, None, :, None] * large_ext[None]
    )
    local_fields = vorticity(velocity, metric)
    pieces = local_fields.reshape(
        own_snaps, 3, local_fields.shape[2], snap_count, block_cols, local_fields.shape[4]
    )
    fields = lax.all_to_all(pieces, "snap", split_axis=3, concat_axis=0, tiled=True)[:, :, :, 0]
    snapshot_rows = fields.reshape(fields.shape[0], -1)
    gram_local = inner_rows(snapshot_rows, snapshot_rows)
    gram_total = lax.psum(gram_local, ("slab", "snap"))
    correlation = gram_total / (snapshot_rows.shape[1] * slab_count * snap_count)
    weights = whitening(correlation)
    result = jnp.dot(weights, snapshot_rows, precision=lax.Precision.HIGHEST)
    return result.reshape(fields.shape)


def solution(mesh):
    return jax.shard_map(
        per_device,
        mesh=mesh,
        in_specs=(
            P("snap", None, "slab", None, None),
            P(None, "slab", None, None),
            P(),
            P(None, "slab", None, None),
        ),
        out_specs=P(None, None, "slab", "snap", None),
        check_vma=False,
    )
```

profile of v0, /device:TPU:1, one launch (start us, length us, event | category | flops | bytes accessed | tf_op | source)
XLA Modules:
  0.0 358.1 jit_solution(2387422955889473556)
XLA Ops:
  6.5 0.0 copy-start
  6.5 0.0 copy-start.2
  6.5 0.0 copy-start.3
  6.5 0.0 all-reduce.2.cloned.1.call-start
  6.5 2.9 fusion.21
  9.4 4.1 %collective-permute-start = (bf16[17,3,1,64,128]{4,3,2,1,0:T(8,128)(2,1)}, bf16[17,3,1,64,128]{4,3,2,1,0:T(8,128)(2,1)S(1)}, u32[]{:S(2)}, u32[]{:S(2)}) collective-permute-start(bf16[17,3,1,64,128]{4,3,2,1,0:T(8,128)(2,1)} %get-tuple-element.20), channel_id=1, source_target_pairs={{0,8},{8,16},{16,24},{24,32},{32,40},{40,48},{48,56},{56,64},{64,7... | collective-permute-start | bytes 2506760 | tf_op jit(solution)/shard_map/ppermute | solution.py:14
  13.5 1.3 collective-permute-start.1
  14.8 0.0 copy-done.3
  14.8 0.1 dynamic-slice_maximum_fusion
  14.9 0.1 copy.10
  15.0 1.0 multiply_bitcast_fusion.2
  15.9 15.1 %collective-permute-done = bf16[17,3,1,64,128]{4,3,2,1,0:T(8,128)(2,1)S(1)} collective-permute-done((bf16[17,3,1,64,128]{4,3,2,1,0:T(8,128)(2,1)}, bf16[17,3,1,64,128]{4,3,2,1,0:T(8,128)(2,1)S(1)}, u32[]{:S(2)}, u32[]{:S(2)}) %collective-permute-start) | collective-permute-done | bytes 835616 | tf_op jit(solution)/shard_map/ppermute | solution.py:14
  31.0 3.8 %collective-permute-done.1 = bf16[17,3,1,64,128]{4,3,2,1,0:T(8,128)(2,1)S(1)} collective-permute-done((bf16[17,3,1,64,128]{4,3,2,1,0:T(8,128)(2,1)}, bf16[17,3,1,64,128]{4,3,2,1,0:T(8,128)(2,1)S(1)}, u32[]{:S(2)}, u32[]{:S(2)}) %collective-permute-start.1) | collective-permute-done | bytes 835616 | tf_op jit(solution)/shard_map/ppermute | solution.py:17
  34.8 0.0 copy-done
  34.8 0.0 copy-done.2
  34.8 0.5 pad_maximum_fusion
  35.3 0.7 slice_convert_fusion
  36.1 0.1 fusion.27
  36.3 1.5 maximum_add_fusion
  37.7 0.5 slice_bitcast_fusion.2
  38.2 0.9 fusion.28
  39.1 0.9 fusion.29
  40.0 0.8 fusion.9
  40.7 1.5 fusion.19
  42.2 0.2 pad_maximum_fusion.1
  42.5 0.3 copy.19
  42.8 43.4 %all_to_all.15 = f32[16,3,2,8,8,128]{5,4,2,1,0,3:T(8,128)} all-to-all(f32[16,3,2,8,8,128]{5,4,2,1,0,3:T(8,128)S(1)} %copy.19), channel_id=1, replica_groups=mesh['slab'=32,'snap'=8] {'snap'}, dimensions={3} | all-to-all | bytes 6291456 | tf_op jit(solution)/shard_map/all_to_all | solution.py:105
  86.2 2.8 reshape_squeeze.3
  89.0 3.2 fusion.34
  92.2 0.0 all-reduce.2.cloned.1.call-update
  92.2 2.4 copy.16
  94.6 0.0 copy-start.1
  94.6 242.7 %all-reduce.2.cloned.1.call-done = f32[128,128]{1,0:T(8,128)} async-done(((f32[128,128]{1,0:T(8,128)}), f32[128,128]{1,0:T(8,128)}) %all-reduce.2.cloned.1.call-update) | async-done | bytes 65552 | tf_op jit(solution)/shard_map/psum | solution.py:108
  337.3 1.5 multiply_reduce_fusion
  339.5 1.0 fusion.6
  340.5 0.2 fusion.23
  340.7 1.0 fusion.24
  341.8 0.2 fusion.5
  342.0 0.2 fusion.36
  342.2 0.2 fusion.35
  342.4 0.2 fusion.4
  342.6 0.2 fusion.38
  342.8 0.2 fusion.37
  343.0 0.2 fusion.3
  343.3 0.2 fusion.40
  343.5 0.2 fusion.39
  343.7 0.2 fusion.2
  343.9 0.2 fusion.41
  344.1 0.2 fusion.42
  344.3 0.2 fusion.1
  344.5 0.2 fusion
  344.7 0.0 copy-done.1
  344.7 3.0 fusion.43
  347.8 3.5 copy.17
  (4 shorter events, 0.1 us)
Async XLA Ops:
  6.5 28.2 %copy-start = (bf16[16,3,2,64,128]{4,3,2,1,0:T(8,128)(2,1)S(1)}, bf16[16,3,2,64,128]{4,3,2,1,0:T(8,128)(2,1)}, u32[]{:S(2)}) copy-start(bf16[16,3,2,64,128]{4,3,2,1,0:T(8,128)(2,1)} %param.4) | copy-start | bytes 4718596
  6.5 28.2 %copy-start.2 = (bf16[3,2,64,128]{3,2,1,0:T(8,128)(2,1)S(1)}, bf16[3,2,64,128]{3,2,1,0:T(8,128)(2,1)}, u32[]{:S(2)}) copy-start(bf16[3,2,64,128]{3,2,1,0:T(8,128)(2,1)} %param.5) | copy-start | bytes 294916
  6.5 8.2 %copy-start.3 = (f32[128,64]{0,1:T(8,128)S(1)}, f32[128,64]{0,1:T(8,128)}, u32[]{:S(2)}) copy-start(f32[128,64]{0,1:T(8,128)} %param.6) | copy-start | bytes 98308
  6.5 330.8 %all-reduce.2.cloned.1.call-start = ((), (), s32[]{:S(2)}) async-start(), calls=%async_computation.1 | async-start | bytes 131072 | tf_op jit(solution)/shard_map/psum | solution.py:108
  9.4 21.6 %collective-permute-start = (bf16[17,3,1,64,128]{4,3,2,1,0:T(8,128)(2,1)}, bf16[17,3,1,64,128]{4,3,2,1,0:T(8,128)(2,1)S(1)}, u32[]{:S(2)}, u32[]{:S(2)}) collective-permute-start(bf16[17,3,1,64,128]{4,3,2,1,0:T(8,128)(2,1)} %get-tuple-element.20), channel_id=1, source_target_pairs={{0,8},{8,16},{16,24},{24,32},{32,40},{40,48},{48,56},{56,64},{64,7... | collective-permute-start | bytes 2506760 | tf_op jit(solution)/shard_map/ppermute | solution.py:14
  13.5 21.3 %collective-permute-start.1 = (bf16[17,3,1,64,128]{4,3,2,1,0:T(8,128)(2,1)}, bf16[17,3,1,64,128]{4,3,2,1,0:T(8,128)(2,1)S(1)}, u32[]{:S(2)}, u32[]{:S(2)}) collective-permute-start(bf16[17,3,1,64,128]{4,3,2,1,0:T(8,128)(2,1)} %get-tuple-element.21), channel_id=1, source_target_pairs={{8,0},{16,8},{24,16},{32,24},{40,32},{48,40},{56,48},{64,56},{72,6... | collective-permute-start | bytes 2506760 | tf_op jit(solution)/shard_map/ppermute | solution.py:17
  94.6 250.2 %copy-start.1 = (f32[6144,128]{1,0:T(8,128)S(1)}, f32[6144,128]{1,0:T(8,128)}, u32[]{:S(2)}) copy-start(f32[6144,128]{1,0:T(8,128)} %copy.16) | copy-start | bytes 9437188
Sparse Core Ops, SparseCore 0:
  92.3 244.9 all-reduce.1
where the time goes:
time: 358 us
  waiting for transfers between devices  262 us (73%)
  blocking collectives  43.4 us (12%)
  between operations  14.4 us (4%)
  local copies, waits for them, and re-layouts  11.3 us (3%)
  matrix products  11.3 us (3%)
  other arithmetic  10.6 us (3%)
  starting transfers between devices  5.35 us (1%)
    psum x1, waiting for transfers between devices, per_device(): gram_total = lax.psum(gram_local, ('slab', 'snap'))  243 us
    all_to_all x1, blocking collectives, per_device(): lax.all_to_all(pieces, 'snap', split_axis=3, concat_axis=0, tiled=True)  43.4 us
    ppermute x1, waiting for transfers between devices, with_halo(): lax.ppermute(lax.slice_in_dim(block, block.shape[dim] - width, None, axis...  15.1 us
  transfers between devices with their start and end apart: 3, of which 3 were waited for; matrix products, arithmetic and copies ran while one was open for 1% of the time, Pallas kernels for 0%

commit v1 on v0

--- a/solution.py
+++ b/solution.py
@@ -1,9 +1,17 @@
+import functools
 import jax
 import jax.numpy as jnp
 from jax import lax
 from jax.sharding import PartitionSpec as P
 
 NSITER = 6
+
+
+def build_members_all(inner_x, peer_axis):
+    return jnp.sum(lax.all_gather(inner_x, axis_name=peer_axis), 0)
+
+
+register_leaves_in = functools.partial(build_members_all, peer_axis=("slab", "snap"))
 
 
 def with_halo(block, sides, width):
@@ -105,7 +113,7 @@
     fields = lax.all_to_all(pieces, "snap", split_axis=3, concat_axis=0, tiled=True)[:, :, :, 0]
     snapshot_rows = fields.reshape(fields.shape[0], -1)
     gram_local = inner_rows(snapshot_rows, snapshot_rows)
-    gram_total = lax.psum(gram_local, ("slab", "snap"))
+    gram_total = register_leaves_in(gram_local)
     correlation = gram_total / (snapshot_rows.shape[1] * slab_count * snap_count)
     weights = whitening(correlation)
     result = jnp.dot(weights, snapshot_rows, precision=lax.Precision.HIGHEST)

time: 358 us -> 247 us (0.69)
  waiting for transfers between devices: 262 us -> 145 us
  other arithmetic: 10.6 us -> 16.4 us
    psum x1 -> x0, waiting for transfers between devices: 243 us -> none  [per_device(): gram_total = lax.psum(gram_local, ('slab', 'snap'))]
    all_gather x0 -> x1, waiting for transfers between devices: none -> 127 us  [build_members_all(): return jnp.sum(lax.all_gather(inner_x, axis_name=peer_axis), 0)]
    reduce_sum x0 -> x1, other arithmetic: none -> 6.59 us  [build_members_all(): return jnp.sum(lax.all_gather(inner_x, axis_name=peer_axis), 0)]
where the time goes in v1:
time: 247 us; the launch traced here: 246 us
  waiting for transfers between devices  145 us (59%)
  blocking collectives  43.4 us (18%)
  other arithmetic  16.4 us (7%)
  between operations  14.7 us (6%)
  local copies, waits for them, and re-layouts  11.3 us (5%)
  matrix products  9.65 us (4%)
  starting transfers between devices  5.35 us (2%)
    all_gather x1, waiting for transfers between devices, build_members_all(): return jnp.sum(lax.all_gather(inner_x, axis_name=peer_axis), 0)  127 us
    all_to_all x1, blocking collectives, per_device(): lax.all_to_all(pieces, 'snap', split_axis=3, concat_axis=0, tiled=True)  43.4 us
    ppermute x1, waiting for transfers between devices, with_halo(): lax.ppermute(lax.slice_in_dim(block, block.shape[dim] - width, None, axis...  15.1 us
    reduce_sum x1, other arithmetic, build_members_all(): return jnp.sum(lax.all_gather(inner_x, axis_name=peer_axis), 0)  6.59 us
    dot_general x2, local copies, waits for them, and re-layouts, per_device(): result = jnp.dot(weights, snapshot_rows, precision=lax.Precision.HIGHEST)  5.85 us
  transfers between devices with their start and end apart: 3, of which 3 were waited for; matrix products, arithmetic and copies ran while one was open for 1% of the time, Pallas kernels for 0%

profile of v1, /device:TPU:1, one launch (start us, length us, event | category | flops | bytes accessed | tf_op | source)
XLA Modules:
  0.0 246.4 jit_solution(129712450595528247)
XLA Ops:
  6.5 0.0 copy-start
  6.5 0.0 copy-start.2
  6.5 0.0 copy-start.3
  6.5 0.0 all-gather.3.cloned.1.call-start
  6.5 2.9 %fusion.21 = (bf16[17,3,1,64,128]{4,3,2,1,0:T(8,128)(2,1)}, bf16[17,3,1,64,128]{4,3,2,1,0:T(8,128)(2,1)}) fusion(bf16[16,3,2,64,128]{4,3,2,1,0:T(8,128)(2,1)} %param.4, bf16[1,3,2,64,128]{4,3,2,1,0:T(8,128)(2,1)} %bitcast.82), kind=kLoop, calls=%fused_computation.44 | loop fusion | flops 835584 | bytes 3342336 | tf_op jit(solution)/shard_map/concatenate | solution.py:91
  9.4 4.1 %collective-permute-start = (bf16[17,3,1,64,128]{4,3,2,1,0:T(8,128)(2,1)}, bf16[17,3,1,64,128]{4,3,2,1,0:T(8,128)(2,1)S(1)}, u32[]{:S(2)}, u32[]{:S(2)}) collective-permute-start(bf16[17,3,1,64,128]{4,3,2,1,0:T(8,128)(2,1)} %get-tuple-element.20), channel_id=1, source_target_pairs={{0,8},{8,16},{16,24},{24,32},{32,40},{40,48},{48,56},{56,64},{64,7... | collective-permute-start | bytes 2506760 | tf_op jit(solution)/shard_map/ppermute | solution.py:22
  13.5 1.3 collective-permute-start.1
  14.8 0.0 copy-done.3
  14.8 0.1 dynamic-slice_maximum_fusion
  14.9 0.1 copy.18
  15.0 1.0 multiply_bitcast_fusion.2
  15.9 15.1 %collective-permute-done = bf16[17,3,1,64,128]{4,3,2,1,0:T(8,128)(2,1)S(1)} collective-permute-done((bf16[17,3,1,64,128]{4,3,2,1,0:T(8,128)(2,1)}, bf16[17,3,1,64,128]{4,3,2,1,0:T(8,128)(2,1)S(1)}, u32[]{:S(2)}, u32[]{:S(2)}) %collective-permute-start) | collective-permute-done | bytes 835616 | tf_op jit(solution)/shard_map/ppermute | solution.py:22
  31.0 3.8 %collective-permute-done.1 = bf16[17,3,1,64,128]{4,3,2,1,0:T(8,128)(2,1)S(1)} collective-permute-done((bf16[17,3,1,64,128]{4,3,2,1,0:T(8,128)(2,1)}, bf16[17,3,1,64,128]{4,3,2,1,0:T(8,128)(2,1)S(1)}, u32[]{:S(2)}, u32[]{:S(2)}) %collective-permute-start.1) | collective-permute-done | bytes 835616 | tf_op jit(solution)/shard_map/ppermute | solution.py:25
  34.8 0.0 copy-done
  34.8 0.0 copy-done.2
  34.8 0.5 pad_maximum_fusion
  35.3 0.7 slice_convert_fusion
  36.1 0.1 fusion.27
  36.3 1.5 maximum_add_fusion
  37.7 0.5 slice_bitcast_fusion.2
  38.2 0.9 fusion.28
  39.1 0.9 fusion.29
  40.0 0.8 fusion.9
  40.7 1.5 fusion.19
  42.2 0.2 pad_maximum_fusion.1
  42.5 0.3 copy.27
  42.8 43.4 %all_to_all.15 = f32[16,3,2,8,8,128]{5,4,2,1,0,3:T(8,128)} all-to-all(f32[16,3,2,8,8,128]{5,4,2,1,0,3:T(8,128)S(1)} %copy.27), channel_id=1, replica_groups=mesh['slab'=32,'snap'=8] {'snap'}, dimensions={3} | all-to-all | bytes 6291456 | tf_op jit(solution)/shard_map/all_to_all | solution.py:113
  86.2 2.8 %reshape_squeeze.3 = f32[128,6144]{1,0:T(8,128)S(1)} reshape(f32[8,16,3,2,1,8,128]{6,5,3,2,1,0,4:T(8,128)} %bitcast.81) | data formatting | bytes 6291456 | tf_op jit(solution)/shard_map/reshape;squeeze | solution.py:114
  89.0 3.2 %fusion.34 = f32[128,128]{1,0:T(8,128)} fusion(f32[128,6144]{1,0:T(8,128)S(1)} %reshape_squeeze.3), kind=kOutput, calls=%fused_computation.69 | convolution fusion | flops 1207959552 | bytes 3211264 | tf_op jit(solution)/shard_map/dot_general | solution.py:81
  92.2 0.0 all-gather.3.cloned.1.call-update
  92.2 2.4 copy.24
  94.6 126.6 %all-gather.3.cloned.1.call-done = f32[32768,128]{1,0:T(8,128)} async-done(((f32[128,128]{1,0:T(8,128)}), f32[32768,128]{1,0:T(8,128)}) %all-gather.3.cloned.1.call-update) | async-done | bytes 16777232 | tf_op jit(solution)/shard_map/all_gather | solution.py:11
  221.2 6.6 %reduce_sum.18 = f32[128,128]{1,0:T(8,128)S(1)} reduce(f32[256,128,128]{2,1,0:T(8,128)} %bitcast.79, f32[]{:T(128)} %constant.10.clone.1), dimensions={0}, to_apply=%region_0.1 | reduce | flops 4177920 | bytes 16842756 | tf_op jit(solution)/shard_map/reduce_sum | solution.py:11
  227.8 0.0 copy-start.1
  227.8 0.6 multiply_reduce_fusion
  229.5 0.2 fusion.6
  229.7 0.2 fusion.24
  229.9 0.2 fusion.23
  230.1 0.2 fusion.5
  230.3 0.2 fusion.36
  230.5 0.2 fusion.35
  230.7 0.2 fusion.4
  230.9 0.2 fusion.38
  231.1 0.2 fusion.37
  231.3 0.2 fusion.3
  231.5 0.2 fusion.40
  231.7 0.2 fusion.39
  232.0 0.2 fusion.2
  232.2 0.2 fusion.41
  232.4 0.2 fusion.42
  232.6 0.2 fusion.1
  232.8 0.2 fusion
  233.0 0.0 copy-done.1
  233.0 3.0 %fusion.43 = f32[128,3,2,8,128]{4,0,3,2,1:T(8,128)S(1)} fusion(f32[128,128,1,1,1]{1,0,4,3,2:T(8,128)S(1)} %fusion, f32[3,2,8,128,128]{4,3,2,1,0:T(8,128)S(1)} %bitcast.80), kind=kOutput, calls=%fused_computation.78 | convolution fusion | flops 1207959552 | bytes 6356992 | tf_op jit(solution)/shard_map/dot_general | solution.py:119
  236.0 3.5 %copy.25 = f32[128,3,2,8,128]{4,3,2,1,0:T(8,128)} copy(f32[128,3,2,8,128]{4,0,3,2,1:T(8,128)S(1)} %fusion.43) | data formatting | bytes 6291456 | tf_op jit(solution)/shard_map/dot_general | solution.py:119
  (4 shorter events, 0.1 us)
Async XLA Ops:
  6.5 28.2 %copy-start = (bf16[16,3,2,64,128]{4,3,2,1,0:T(8,128)(2,1)S(1)}, bf16[16,3,2,64,128]{4,3,2,1,0:T(8,128)(2,1)}, u32[]{:S(2)}) copy-start(bf16[16,3,2,64,128]{4,3,2,1,0:T(8,128)(2,1)} %param.4) | copy-start | bytes 4718596
  6.5 28.2 %copy-start.2 = (bf16[3,2,64,128]{3,2,1,0:T(8,128)(2,1)S(1)}, bf16[3,2,64,128]{3,2,1,0:T(8,128)(2,1)}, u32[]{:S(2)}) copy-start(bf16[3,2,64,128]{3,2,1,0:T(8,128)(2,1)} %param.5) | copy-start | bytes 294916
  6.5 8.2 %copy-start.3 = (f32[128,64]{0,1:T(8,128)S(1)}, f32[128,64]{0,1:T(8,128)}, u32[]{:S(2)}) copy-start(f32[128,64]{0,1:T(8,128)} %param.6) | copy-start | bytes 98308
  6.5 214.7 %all-gather.3.cloned.1.call-start = ((), (), s32[]{:S(2)}) async-start(), calls=%async_computation.1 | async-start | bytes 16842752 | tf_op jit(solution)/shard_map/all_gather | solution.py:11
  9.4 21.6 %collective-permute-start = (bf16[17,3,1,64,128]{4,3,2,1,0:T(8,128)(2,1)}, bf16[17,3,1,64,128]{4,3,2,1,0:T(8,128)(2,1)S(1)}, u32[]{:S(2)}, u32[]{:S(2)}) collective-permute-start(bf16[17,3,1,64,128]{4,3,2,1,0:T(8,128)(2,1)} %get-tuple-element.20), channel_id=1, source_target_pairs={{0,8},{8,16},{16,24},{24,32},{32,40},{40,48},{48,56},{56,64},{64,7... | collective-permute-start | bytes 2506760 | tf_op jit(solution)/shard_map/ppermute | solution.py:22
  13.5 21.3 %collective-permute-start.1 = (bf16[17,3,1,64,128]{4,3,2,1,0:T(8,128)(2,1)}, bf16[17,3,1,64,128]{4,3,2,1,0:T(8,128)(2,1)S(1)}, u32[]{:S(2)}, u32[]{:S(2)}) collective-permute-start(bf16[17,3,1,64,128]{4,3,2,1,0:T(8,128)(2,1)} %get-tuple-element.21), channel_id=1, source_target_pairs={{8,0},{16,8},{24,16},{32,24},{40,32},{48,40},{56,48},{64,56},{72,6... | collective-permute-start | bytes 2506760 | tf_op jit(solution)/shard_map/ppermute | solution.py:25
  227.8 5.2 %copy-start.1 = (f32[6144,128]{1,0:T(8,128)S(1)}, f32[6144,128]{1,0:T(8,128)}, u32[]{:S(2)}) copy-start(f32[6144,128]{1,0:T(8,128)} %copy.24) | copy-start | bytes 9437188
Sparse Core Ops, SparseCore 0:
  92.3 128.8 all-gather.2
